TPU v7x, 256 devices: a whole 4x4x8 slice. The times are simulated.
256 devices in a mesh: sec: 32 (over z, y), blk: 8 (over x, core).
Axes of the slice: x: 4, y: 4, z: 8, core: 2. Of those that a mesh axis runs over, the one named last changes fastest.
Arguments:
- state_now: float32 [128, 65536], P(None, ('sec', 'blk')), may hold values from -5 to 5
- source: float32 [128, 65536], P(None, ('sec', 'blk')), may hold values from -6 to 6
- fan_gain: float32 [65536], P(('sec', 'blk')), may hold values from 0.5 to 12
- section_block: bfloat16 [65536, 2048], P(('sec', 'blk')), may hold values from -1 to 7
- block_inverse: bfloat16 [65536, 2048], P(('sec', 'blk')), may hold values from -1 to 1
- back_panel: bfloat16 [65536, 128], P(('sec', 'blk')), may hold values from -6 to 6
- ahead_panel: bfloat16 [65536, 128], P(('sec', 'blk')), may hold values from -0.0625 to 0.0625
- interface: int32 [32, 128], P('sec'), may hold values from 0 to 2047, as said below
Outputs:
- new_state: float32 [128, 65536], P(None, ('sec', 'blk'))
Inputs may be any that keep to these rules, and one draw needn't show every extreme that they name: `interface`: entries of one section are distinct; entry p lies in [p * 16, (p + 1) * 16).
All inputs are finite; a program needn't handle non-finite values.
Results may differ from a plain program's by a relative error of at most 0.0063.
Values may be sent and summed in bfloat16 or wider, within the bound.
A program may use at most 64 MiB of HBM per device.

v0:
```python
import jax
import jax.numpy as jnp
from jax import lax
from jax.sharding import PartitionSpec as P

KRYLOV = 3
epsilon = 1e-06


def extended(x, sides, width):
    for axis, dim in sides:
        size, length = (lax.axis_size(axis), x.shape[dim])
        up = [(i, (i + 1) % size) for i in range(size - 1)]
        down = [(j, i) for i, j in up]
        last = lax.slice_in_dim(x, length - width, length, axis=dim)
        first = lax.slice_in_dim(x, 0, width, axis=dim)
        before = lax.ppermute(last, axis, up)
        after = lax.ppermute(first, axis, down)
        x = jnp.concatenate([before, x, after], axis=dim)
    return x


def entering(value, axis, join, neutral):
    count, mine = (lax.axis_size(axis), lax.axis_index(axis))
    pieces = jax.tree.map(lambda part: lax.all_gather(part, axis), value)
    so_far = jax.tree.map(
        lambda part, zero: jnp.full_like(part, 0) + jnp.asarray(zero, part.dtype), value, neutral
    )

    def step(position, so_far):
        longer = join(so_far, jax.tree.map(lambda part: part[position], pieces))
        return jax.tree.map(lambda new, old: jnp.where(position < mine, new, old), longer, so_far)

    return lax.fori_loop(0, count - 1, step, so_far)


def least_squares(hessen, beta):
    cases = hessen.shape[0]
    depth = hessen.shape[2]
    rhs = jnp.zeros((cases, depth + 1), jnp.float32).at[:, 0].set(beta)
    upper = hessen
    for column in range(depth):
        upper_row = upper[:, column, :]
        lower_row = upper[:, column + 1, :]
        radius = jnp.sqrt(upper_row[:, column] ** 2 + lower_row[:, column] ** 2)
        cosine = upper_row[:, column] / radius
        sine_term = lower_row[:, column] / radius
        upper = upper.at[:, column, :].set(
            cosine[:, None] * upper_row + sine_term[:, None] * lower_row
        )
        upper = upper.at[:, column + 1, :].set(
            -sine_term[:, None] * upper_row + cosine[:, None] * lower_row
        )
        first_rhs = rhs[:, column]
        second_rhs = rhs[:, column + 1]
        rhs = rhs.at[:, column].set(cosine * first_rhs + sine_term * second_rhs)
        rhs = rhs.at[:, column + 1].set(-sine_term * first_rhs + cosine * second_rhs)
    weights = jnp.zeros((cases, depth), jnp.float32)
    for column in reversed(range(depth)):
        remain = rhs[:, column] - jnp.sum(
            upper[:, column, column + 1 :] * weights[:, column + 1 :], axis=1
        )
        weights = weights.at[:, column].set(remain / upper[:, column, column])
    return weights


def local(
    state_now, source, fan_gain, section_block, block_inverse, back_panel, ahead_panel, interface
):
    highest = lax.Precision.HIGHEST
    cases, node_rows = state_now.shape
    panel_width = back_panel.shape[1]
    indices = interface[0]
    first_row = lax.axis_index("blk") * node_rows
    selector = (indices[None, :] == first_row + jnp.arange(node_rows)[:, None]).astype(jnp.float32)
    contract = (((1,), (1,)), ((), ()))
    gain_panel = jnp.dot(
        block_inverse,
        lax.all_gather(back_panel, "blk", axis=0, tiled=True),
        preferred_element_type=jnp.float32,
    )
    panel_maps = -lax.psum(jnp.dot(selector.T, gain_panel, precision=highest), "blk")

    def section_terms(dense_part, behind_vals, piece):
        width = piece.shape[1]
        dense_part = lax.dot_general(
            piece, section_block, contract, preferred_element_type=jnp.float32
        )
        picker = (indices[None, :] == jnp.arange(width)[:, None]).astype(jnp.bfloat16)
        behind_vals = jnp.dot(piece, picker, preferred_element_type=jnp.float32)
        return (dense_part, behind_vals)

    def fold_section(carry, piece):
        return section_terms(carry[0], carry[1], piece)

    def operator(vector):
        rounded = vector.astype(jnp.bfloat16)
        empty_dense = jnp.zeros((cases, node_rows), jnp.float32)
        empty_panel = jnp.zeros((cases, panel_width), jnp.float32)
        start_carry = (empty_dense, empty_panel)
        folded = fold_section(start_carry, lax.all_gather(rounded, "blk", axis=1, tiled=True))
        dense_part, behind_vals = folded
        upward = lax.psum(jnp.dot(rounded, ahead_panel, preferred_element_type=jnp.float32), "blk")
        framed = extended(jnp.stack([behind_vals, upward])[None], (("sec", 0),), 1)
        behind = framed[0, 0].astype(jnp.bfloat16)
        ahead_term = framed[2, 1]
        lower_term = lax.dot_general(
            behind, back_panel, contract, preferred_element_type=jnp.float32
        )
        upper_term = jnp.dot(ahead_term, selector.T, precision=highest)
        return dense_part + lower_term + upper_term

    def compose(earlier, later):
        first_map, first_value = earlier
        second_map, second_value = later
        joined_map = jnp.dot(second_map, first_map, precision=highest)
        joined_value = jnp.dot(first_value, second_map.T, precision=highest) + second_value
        return (joined_map, joined_value)

    def lengths(vector):
        return jnp.sqrt(lax.psum(jnp.sum(vector * vector, axis=1), ("sec", "blk")) + epsilon)

    bent = jnp.tanh(state_now)
    residual = source - operator(state_now) - fan_gain[None, :] * bent
    jac_diag = fan_gain[None, :] * (1.0 - bent * bent)
    beta = lengths(residual)
    basis = [residual / beta[:, None]]
    directions = []
    hessen = jnp.zeros((cases, KRYLOV + 1, KRYLOV), jnp.float32)
    for column in range(KRYLOV):
        precondition_rounded = basis[column].astype(jnp.bfloat16)
        precondition_folded = lax.dot_general(
            lax.all_gather(precondition_rounded, "blk", axis=1, tiled=True),
            block_inverse,
            contract,
            preferred_element_type=jnp.float32,
        )
        values = lax.psum(jnp.dot(precondition_folded, selector, precision=highest), "blk")
        identity = (
            jnp.eye(panel_width, dtype=jnp.float32),
            jnp.zeros((cases, panel_width), jnp.float32),
        )
        _, before = entering((panel_maps, values), "sec", compose, identity)
        direction = precondition_folded - lax.dot_general(
            before, gain_panel, contract, precision=highest
        )
        product = operator(direction) + jac_diag * direction
        stacked = jnp.stack(basis)
        projections = lax.psum(jnp.sum(product[None] * stacked, axis=2), ("sec", "blk"))
        product = product - jnp.sum(projections[:, :, None] * stacked, axis=0)
        length = lengths(product)
        hessen = hessen.at[:, : column + 1, column].set(projections.T)
        hessen = hessen.at[:, column + 1, column].set(length)
        basis.append(product / length[:, None])
        directions.append(direction)
    weights = least_squares(hessen, beta)
    update = jnp.zeros_like(state_now)
    for column in range(KRYLOV):
        update = update + weights[:, column : column + 1] * directions[column]
    return state_now + update


def solution(mesh):
    in_specs = (
        P(None, ("sec", "blk")),
        P(None, ("sec", "blk")),
        P(("sec", "blk")),
        P(("sec", "blk"), None),
        P(("sec", "blk"), None),
        P(("sec", "blk"), None),
        P(("sec", "blk"), None),
        P("sec", None),
    )
    out_specs = P(None, ("sec", "blk"))
    return jax.shard_map(local, mesh=mesh, in_specs=in_specs, out_specs=out_specs, check_vma=False)
```

profile of v0, /device:TPU:1, one launch (start us, length us, event | category | flops | bytes accessed | tf_op | source)
XLA Modules:
  0.0 1640.1 jit_solution(12427240941463223437)
XLA Ops:
  6.5 1.1 convert_element_type.42
  7.6 1.7 convolution_bitcast_fusion.13
  9.4 16.2 all_gather.52
  27.1 13.1 all_gather.54
  40.7 34.6 %all-reduce.11.cloned.1.call-done = f32[1,128,128]{1,2,0:T(8,128)} async-done(((f32[1,128,128]{1,2,0:T(8,128)}), f32[1,128,128]{1,2,0:T(8,128)}) %all-reduce.11.cloned.1.call-update) | async-done | bytes 65552 | tf_op jit(solution)/shard_map/psum | solution.py:103
  76.1 3.1 collective-permute-start
  80.2 1.3 collective-permute-start.1
  81.7 4.2 collective-permute-done.1
  86.3 83.2 %psum.106 = f32[128]{0:T(128)S(1)} all-reduce(f32[128]{0:T(128)S(1)} %get-tuple-element.720), channel_id=1, replica_groups=mesh['sec'=32,'blk'=8] {'sec','blk'}, use_global_device_ids=true, to_apply=%region_4.0 | all-reduce | flops 128 | bytes 1024 | tf_op jit(solution)/shard_map/psum | solution.py:121
  169.7 13.9 all_gather.53
  185.0 57.8 %all-reduce.23.cloned.1.call-done = (f32[128,128]{1,0:T(8,128)}, f32[1,128,128]{2,1,0:T(8,128)}) async-done(((f32[128,128]{1,0:T(8,128)}, f32[1,128,128]{2,1,0:T(8,128)}), (f32[128,128]{1,0:T(8,128)}, f32[1,128,128]{2,1,0:T(8,128)})) %all-reduce.23.cloned.1.call-update) | async-done | bytes 131088 | tf_op jit(solution)/shard_map/psum | solution.py:82
  242.8 1.5 neg.24
  244.9 75.7 %all-gather.12.cloned.1.call-done = f32[4096,128]{1,0:T(8,128)} async-done(((f32[128,128]{1,0:T(8,128)}), f32[4096,128]{1,0:T(8,128)}) %all-gather.12.cloned.1.call-update) | async-done | bytes 2097168 | tf_op jit(solution)/shard_map/all_gather | solution.py:25
  320.6 77.6 %all-gather.6.cloned.1.call-done = f32[32,128,128]{2,1,0:T(8,128)} async-done(((f32[1,128,128]{2,1,0:T(8,128)}), f32[32,128,128]{2,1,0:T(8,128)}) %all-gather.6.cloned.1.call-update) | async-done | bytes 2097168 | tf_op jit(solution)/shard_map/all_gather | solution.py:25
  398.3 63.2 %while.64 = (s32[]{:T(128)}, f32[128,128]{0,1:T(8,128)S(1)}, s32[]{:T(128)}, f32[32,128,128]{2,1,0:T(8,128)}, f32[32,128,128]{2,1,0:T(8,128)}, /*index=5*/s32[]{:T(128)}, s32[]{:T(128)}) while((s32[]{:T(128)}, f32[128,128]{0,1:T(8,128)S(1)}, s32[]{:T(128)}, f32[32,128,128]{2,1,0:T(8,128)}, f32[32,128,128]{2,1,0:T(8,128)}, ...), condition=%wide.region_8.9_spmd.clone, body=%wide.region_7.8_spmd.clone.sunk | while | flops 25231364 | bytes 723043 | solution.py:34
  399.3 1.1 fusion.161
  413.5 1.1 fusion.161
  415.6 1.1 fusion.161
  429.8 1.1 fusion.161
  431.9 1.1 fusion.161
  446.1 1.1 fusion.161
  461.8 17.8 %all_gather.59 = bf16[128,2048]{1,0:T(8,128)(2,1)S(1)} all-gather(bf16[128,256]{1,0:T(8,128)(2,1)S(1)} %get-tuple-element.722), channel_id=1, replica_groups=mesh['sec'=32,'blk'=8] {'blk'}, dimensions={1}, use_global_device_ids=true | all-gather | bytes 589824 | tf_op jit(solution)/shard_map/all_gather | solution.py:101
  480.8 57.6 %all-reduce.13.cloned.1.call-done = f32[1,128,128]{2,1,0:T(8,128)} async-done(((f32[1,128,128]{2,1,0:T(8,128)}), f32[1,128,128]{2,1,0:T(8,128)}) %all-reduce.13.cloned.1.call-update) | async-done | bytes 65552 | tf_op jit(solution)/shard_map/psum | solution.py:103
  539.3 3.1 collective-permute-start.2
  542.9 1.3 collective-permute-start.3
  544.4 4.2 collective-permute-done.3
  549.1 83.2 %psum.110 = f32[1,128]{1,0:T(1,128)S(1)} all-reduce(f32[1,128]{1,0:T(1,128)S(1)} %bitcast.287), channel_id=1, replica_groups=mesh['sec'=32,'blk'=8] {'sec','blk'}, use_global_device_ids=true, to_apply=%region_11.12 | all-reduce | flops 128 | bytes 1024 | tf_op jit(solution)/shard_map/psum | solution.py:149
  632.5 72.3 %psum.111 = f32[128]{0:T(128)S(1)} all-reduce(f32[128]{0:T(128)S(1)} %get-tuple-element.687), channel_id=1, replica_groups=mesh['sec'=32,'blk'=8] {'sec','blk'}, use_global_device_ids=true, to_apply=%region_13.14 | all-reduce | flops 128 | bytes 1024 | tf_op jit(solution)/shard_map/psum | solution.py:121
  705.0 13.6 all_gather.60
  720.1 58.5 %all-reduce.15.cloned.1.call-done = f32[1,128,128]{2,1,0:T(8,128)} async-done(((f32[1,128,128]{2,1,0:T(8,128)}), f32[1,128,128]{2,1,0:T(8,128)}) %all-reduce.15.cloned.1.call-update) | async-done | bytes 65552 | tf_op jit(solution)/shard_map/psum | solution.py:138
  778.7 77.7 %all-gather.8.cloned.1.call-done = f32[32,128,128]{2,1,0:T(8,128)} async-done(((f32[1,128,128]{2,1,0:T(8,128)}), f32[32,128,128]{2,1,0:T(8,128)}) %all-gather.8.cloned.1.call-update) | async-done | bytes 2097168 | tf_op jit(solution)/shard_map/all_gather | solution.py:25
  856.4 63.2 %while.65 = (s32[]{:T(128)}, f32[128,128]{0,1:T(8,128)S(1)}, s32[]{:T(128)}, f32[32,128,128]{2,1,0:T(8,128)}, f32[32,128,128]{2,1,0:T(8,128)}, /*index=5*/s32[]{:T(128)}, s32[]{:T(128)}) while((s32[]{:T(128)}, f32[128,128]{0,1:T(8,128)S(1)}, s32[]{:T(128)}, f32[32,128,128]{2,1,0:T(8,128)}, f32[32,128,128]{2,1,0:T(8,128)}, ...), condition=%wide.region_16.17_spmd.clone, body=%wide.region_15.16_spmd.clone.sunk | while | flops 25231364 | bytes 723043 | solution.py:34
  863.4 1.1 fusion.164
  871.6 1.1 fusion.164
  879.8 1.1 fusion.164
  887.9 1.1 fusion.164
  896.1 1.1 fusion.164
  904.2 1.1 fusion.164
  912.4 1.1 fusion.164
  920.6 17.8 %all_gather.63 = bf16[128,2048]{1,0:T(8,128)(2,1)S(1)} all-gather(bf16[128,256]{1,0:T(8,128)(2,1)S(1)} %get-tuple-element.724), channel_id=1, replica_groups=mesh['sec'=32,'blk'=8] {'blk'}, dimensions={1}, use_global_device_ids=true | all-gather | bytes 589824 | tf_op jit(solution)/shard_map/all_gather | solution.py:101
  939.7 57.4 %all-reduce.17.cloned.1.call-done = f32[1,128,128]{2,1,0:T(8,128)} async-done(((f32[1,128,128]{2,1,0:T(8,128)}), f32[1,128,128]{2,1,0:T(8,128)}) %all-reduce.17.cloned.1.call-update) | async-done | bytes 65552 | tf_op jit(solution)/shard_map/psum | solution.py:103
  998.0 3.1 collective-permute-start.4
  1001.6 1.3 collective-permute-start.5
  1003.1 4.2 collective-permute-done.5
  1007.8 83.2 %psum.114 = f32[2,128]{1,0:T(2,128)S(1)} all-reduce(f32[2,128]{1,0:T(2,128)S(1)} %multiply_reduce_fusion.3), channel_id=1, replica_groups=mesh['sec'=32,'blk'=8] {'sec','blk'}, use_global_device_ids=true, to_apply=%region_19.20 | all-reduce | flops 256 | bytes 2048 | tf_op jit(solution)/shard_map/psum | solution.py:149
  1091.2 72.3 %psum.115 = f32[128]{0:T(128)S(1)} all-reduce(f32[128]{0:T(128)S(1)} %get-tuple-element.683), channel_id=1, replica_groups=mesh['sec'=32,'blk'=8] {'sec','blk'}, use_global_device_ids=true, to_apply=%region_22.23 | all-reduce | flops 128 | bytes 1024 | tf_op jit(solution)/shard_map/psum | solution.py:121
  1163.7 13.6 all_gather.64
  1178.8 58.5 %all-reduce.19.cloned.1.call-done = f32[1,128,128]{2,1,0:T(8,128)} async-done(((f32[1,128,128]{2,1,0:T(8,128)}), f32[1,128,128]{2,1,0:T(8,128)}) %all-reduce.19.cloned.1.call-update) | async-done | bytes 65552 | tf_op jit(solution)/shard_map/psum | solution.py:138
  1242.6 1.2 scatter.30
  1243.8 71.1 %all-gather.10.cloned.1.call-done = f32[32,128,128]{2,1,0:T(8,128)} async-done(((f32[1,128,128]{2,1,0:T(8,128)}), f32[32,128,128]{2,1,0:T(8,128)}) %all-gather.10.cloned.1.call-update) | async-done | bytes 2097168 | tf_op jit(solution)/shard_map/all_gather | solution.py:25
  1314.9 63.2 %while.66 = (s32[]{:T(128)}, f32[128,128]{0,1:T(8,128)S(1)}, s32[]{:T(128)}, f32[32,128,128]{2,1,0:T(8,128)}, f32[32,128,128]{2,1,0:T(8,128)}, /*index=5*/s32[]{:T(128)}, s32[]{:T(128)}) while((s32[]{:T(128)}, f32[128,128]{0,1:T(8,128)S(1)}, s32[]{:T(128)}, f32[32,128,128]{2,1,0:T(8,128)}, f32[32,128,128]{2,1,0:T(8,128)}, ...), condition=%wide.region_26.27_spmd.clone, body=%wide.region_25.26_spmd.clone.sunk | while | flops 25231364 | bytes 723043 | solution.py:34
  1379.1 17.8 %all_gather.67 = bf16[128,2048]{1,0:T(8,128)(2,1)S(1)} all-gather(bf16[128,256]{1,0:T(8,128)(2,1)S(1)} %get-tuple-element.726), channel_id=1, replica_groups=mesh['sec'=32,'blk'=8] {'blk'}, dimensions={1}, use_global_device_ids=true | all-gather | bytes 589824 | tf_op jit(solution)/shard_map/all_gather | solution.py:101
  1398.0 57.6 %all-reduce.21.cloned.1.call-done = f32[1,128,128]{2,1,0:T(8,128)} async-done(((f32[1,128,128]{2,1,0:T(8,128)}), f32[1,128,128]{2,1,0:T(8,128)}) %all-reduce.21.cloned.1.call-update) | async-done | bytes 65552 | tf_op jit(solution)/shard_map/psum | solution.py:103
  1456.6 3.2 collective-permute-start.6
  1460.3 1.3 collective-permute-start.7
  1461.8 4.2 collective-permute-done.7
  1467.2 83.2 %psum.118 = f32[3,128]{1,0:T(4,128)S(1)} all-reduce(f32[3,128]{1,0:T(4,128)S(1)} %multiply_reduce_fusion.1), channel_id=1, replica_groups=mesh['sec'=32,'blk'=8] {'sec','blk'}, use_global_device_ids=true, to_apply=%region_29.30 | all-reduce | flops 384 | bytes 3072 | tf_op jit(solution)/shard_map/psum | solution.py:149
  1550.6 72.3 %psum.119 = f32[128]{0:T(128)S(1)} all-reduce(f32[128]{0:T(128)S(1)} %multiply_reduce_fusion.4), channel_id=1, replica_groups=mesh['sec'=32,'blk'=8] {'sec','blk'}, use_global_device_ids=true, to_apply=%region_32.33 | all-reduce | flops 128 | bytes 1024 | tf_op jit(solution)/shard_map/psum | solution.py:121
  1623.0 1.9 broadcast_select_fusion
  1624.9 1.3 scatter.34
  1626.4 1.8 fusion.80
  1628.2 1.8 broadcast_select_fusion.2
  1630.1 1.8 fusion.76
  1631.9 1.7 add_add_fusion
  (489 shorter events, 200.4 us)
Async XLA Ops:
  6.5 33.7 %copy-start = (bf16[256,2048]{1,0:T(8,128)(2,1)S(1)}, bf16[256,2048]{1,0:T(8,128)(2,1)}, u32[]{:S(2)}) copy-start(bf16[256,2048]{1,0:T(8,128)(2,1)} %param.62) | copy-start | bytes 3145732
  6.5 20.0 %copy-start.1 = (bf16[256,2048]{1,0:T(8,128)(2,1)S(1)}, bf16[256,2048]{1,0:T(8,128)(2,1)}, u32[]{:S(2)}) copy-start(bf16[256,2048]{1,0:T(8,128)(2,1)} %param.61) | copy-start | bytes 3145732
  6.5 20.6 %copy-start.3 = (bf16[256,128]{1,0:T(8,128)(2,1)S(1)}, bf16[256,128]{1,0:T(8,128)(2,1)}, u32[]{:S(2)}) copy-start(bf16[256,128]{1,0:T(8,128)(2,1)} %param.63) | copy-start | bytes 196612
  6.5 68.7 %all-reduce.11.cloned.1.call-start = ((), (), s32[]{:S(2)}) async-start(), calls=%async_computation | async-start | bytes 131072 | tf_op jit(solution)/shard_map/psum | solution.py:103
  9.3 233.5 %all-reduce.23.cloned.1.call-start = ((), (), s32[]{:S(2)}) async-start(), calls=%async_computation.10 | async-start | bytes 262144 | tf_op jit(solution)/shard_map/psum | solution.py:82
  26.6 52.7 %copy-start.9 = (s32[1,128]{1,0:T(1,128)S(1)}, s32[1,128]{1,0:T(1,128)}, u32[]{:S(2)}) copy-start(s32[1,128]{1,0:T(1,128)} %param.65) | copy-start | bytes 1540
  26.6 59.3 %copy-start.2 = (f32[128,256]{1,0:T(8,128)S(1)}, f32[128,256]{1,0:T(8,128)}, u32[]{:S(2)}) copy-start(f32[128,256]{1,0:T(8,128)} %param.58) | copy-start | bytes 393220
  26.6 59.3 %copy-start.8 = (f32[128,256]{1,0:T(8,128)S(1)}, f32[128,256]{1,0:T(8,128)}, u32[]{:S(2)}) copy-start(f32[128,256]{1,0:T(8,128)} %param.59) | copy-start | bytes 393220
  26.6 59.3 %copy-start.10 = (f32[256]{0:T(256)S(1)}, f32[256]{0:T(256)}, u32[]{:S(2)}) copy-start(f32[256]{0:T(256)} %param.60) | copy-start | bytes 3076
  76.1 5.4 collective-permute-start
  80.2 5.7 collective-permute-start.1
  169.6 228.7 %copy-start.11 = (f32[128]{0:T(128)}, f32[128]{0:T(128)S(1)}, u32[]{:S(2)}) copy-start(f32[128]{0:T(128)S(1)} %psum.106) | copy-start | bytes 1540
  185.0 135.7 %all-gather.12.cloned.1.call-start = ((), (), s32[]{:S(2)}) async-start(), calls=%async_computation.9 | async-start | bytes 2162688 | tf_op jit(solution)/shard_map/all_gather | solution.py:25
  244.3 154.0 %all-gather.6.cloned.1.call-start = ((), (), s32[]{:S(2)}) async-start(), calls=%async_computation.1 | async-start | bytes 2162688 | tf_op jit(solution)/shard_map/all_gather | solution.py:25
  244.9 293.6 %all-reduce.13.cloned.1.call-start = ((), (), s32[]{:S(2)}) async-start(), calls=%async_computation.2 | async-start | bytes 131072 | tf_op jit(solution)/shard_map/psum | solution.py:103
  398.3 81.4 %copy-start.7 = (bf16[256,128]{1,0:T(8,128)(2,1)S(1)}, bf16[256,128]{1,0:T(8,128)(2,1)}, u32[]{:S(2)}) copy-start(bf16[256,128]{1,0:T(8,128)(2,1)} %param.64) | copy-start | bytes 196612
  480.4 298.2 %all-reduce.15.cloned.1.call-start = ((), (), s32[]{:S(2)}) async-start(), calls=%async_computation.3 | async-start | bytes 131072 | tf_op jit(solution)/shard_map/psum | solution.py:138
  539.3 4.9 collective-permute-start.2
  542.9 5.7 collective-permute-start.3
  720.0 136.3 %all-gather.8.cloned.1.call-start = ((), (), s32[]{:S(2)}) async-start(), calls=%async_computation.4 | async-start | bytes 2162688 | tf_op jit(solution)/shard_map/all_gather | solution.py:25
  778.6 218.5 %all-reduce.17.cloned.1.call-start = ((), (), s32[]{:S(2)}) async-start(), calls=%async_computation.5 | async-start | bytes 131072 | tf_op jit(solution)/shard_map/psum | solution.py:103
  939.1 298.2 %all-reduce.19.cloned.1.call-start = ((), (), s32[]{:S(2)}) async-start(), calls=%async_computation.6 | async-start | bytes 131072 | tf_op jit(solution)/shard_map/psum | solution.py:138
  997.1 10.2 copy-start.4
  998.0 4.9 collective-permute-start.4
  1001.6 5.7 collective-permute-start.5
  1178.8 136.2 %all-gather.10.cloned.1.call-start = ((), (), s32[]{:S(2)}) async-start(), calls=%async_computation.7 | async-start | bytes 2162688 | tf_op jit(solution)/shard_map/all_gather | solution.py:25
  1237.3 218.3 %all-reduce.21.cloned.1.call-start = ((), (), s32[]{:S(2)}) async-start(), calls=%async_computation.8 | async-start | bytes 131072 | tf_op jit(solution)/shard_map/psum | solution.py:103
  1455.7 10.3 copy-start.6
  1456.6 175.3 %copy-start.5 = (f32[128,256]{1,0:T(8,128)S(1)}, f32[128,256]{1,0:T(8,128)}, u32[]{:S(2)}) copy-start(f32[128,256]{1,0:T(8,128)} %get-tuple-element.725) | copy-start | bytes 393220
  1456.6 5.0 collective-permute-start.6
  1460.3 5.7 collective-permute-start.7
Sparse Core Ops, SparseCore 0:
  9.7 65.5 all-reduce.10
  185.1 57.6 all-reduce.22
  245.4 75.2 all-gather.11
  323.1 75.1 all-gather.5
  480.5 57.8 all-reduce.12
  720.2 58.4 all-reduce.14
  781.2 75.1 all-gather.7
  939.3 57.8 all-reduce.16
  1178.9 58.4 all-reduce.18
  1239.8 75.1 all-gather.9
  1397.8 57.8 all-reduce.20
where the time goes:
time: 1650 us; the launch traced here: 1640 us
  waiting for transfers between devices  702 us (43%)
  blocking collectives  674 us (41%)
  matrix products  116 us (7%)
  local copies, waits for them, and re-layouts  91.5 us (6%)
  other arithmetic  20.7 us (1%)
  starting transfers between devices  18.2 us (1%)
    all_gather x4, waiting for transfers between devices, entering(): pieces = jax.tree.map(lambda part: lax.all_gather(part, axis), value)  302 us
    psum x4, blocking collectives, lengths(): lax.psum(jnp.sum(vector * vector, axis=1), ('sec', 'blk')) + epsilon  300 us
    psum x3, blocking collectives, local(): lax.psum(jnp.sum(product[None] * stacked, axis=2), ('sec', 'blk'))  250 us
    psum x4, waiting for transfers between devices, operator(): lax.psum(jnp.dot(rounded, ahead_panel, preferred_element_type=jnp.float32...  207 us
    psum x2, waiting for transfers between devices, local(): lax.psum(jnp.dot(precondition_folded, selector, precision=highest), 'blk')  117 us
    dot_general x93, matrix products, compose(): jnp.dot(first_value, second_map.T, precision=highest) + second_value  97.7 us
    dynamic_slice x186, local copies, waits for them, and re-layouts, step(): longer = join(so_far, jax.tree.map(lambda part: part[position], pieces))  87 us
    all_gather x4, blocking collectives, operator(): lax.all_gather(rounded, 'blk', axis=1, tiled=True)  69.6 us
  transfers between devices with their start and end apart: 19, of which 15 were waited for; matrix products, arithmetic and copies ran while one was open for 1% of the time, Pallas kernels for 0%

commit v1 on v0

--- a/solution.py
+++ b/solution.py
@@ -118,7 +118,9 @@
         return (joined_map, joined_value)
 
     def lengths(vector):
-        return jnp.sqrt(lax.psum(jnp.sum(vector * vector, axis=1), ("sec", "blk")) + epsilon)
+        return jnp.sqrt(
+            lax.psum(lax.psum(jnp.sum(vector * vector, axis=1), "sec"), "blk") + epsilon
+        )
 
     bent = jnp.tanh(state_now)
     residual = source - operator(state_now) - fan_gain[None, :] * bent

time: 1650 us -> 1690 us (1.024)
  blocking collectives: 674 us -> 710 us
    psum x4 -> x8, blocking collectives: 300 us -> 337 us  [the longest x4 227 us: lengths(): lax.psum(jnp.sum(vector * vector, axis=1), 'sec')]
where the time goes in v1:
time: 1690 us; the launch traced here: 1680 us
  blocking collectives  710 us (42%)
  waiting for transfers between devices  705 us (42%)
  matrix products  116 us (7%)
  local copies, waits for them, and re-layouts  91.5 us (5%)
  other arithmetic  20.7 us (1%)
  starting transfers between devices  18 us (1%)
    all_gather x4, waiting for transfers between devices, entering(): pieces = jax.tree.map(lambda part: lax.all_gather(part, axis), value)  302 us
    psum x3, blocking collectives, local(): lax.psum(jnp.sum(product[None] * stacked, axis=2), ('sec', 'blk'))  250 us
    psum x4, blocking collectives, lengths(): lax.psum(jnp.sum(vector * vector, axis=1), 'sec')  227 us
    psum x4, waiting for transfers between devices, operator(): lax.psum(jnp.dot(rounded, ahead_panel, preferred_element_type=jnp.float32...  207 us
    psum x2, waiting for transfers between devices, local(): lax.psum(jnp.dot(precondition_folded, selector, precision=highest), 'blk')  116 us
    psum x4, blocking collectives, lengths(): lax.psum(lax.psum(jnp.sum(vector * vector, axis=1), 'sec'), 'blk') + epsilon  110 us
    dot_general x93, matrix products, compose(): jnp.dot(first_value, second_map.T, precision=highest) + second_value  97.7 us
    dynamic_slice x186, local copies, waits for them, and re-layouts, step(): longer = join(so_far, jax.tree.map(lambda part: part[position], pieces))  87 us
  transfers between devices with their start and end apart: 19, of which 15 were waited for; matrix products, arithmetic and copies ran while one was open for 1% of the time, Pallas kernels for 0%

profile of v1, /device:TPU:1, one launch (start us, length us, event | category | flops | bytes accessed | tf_op | source)
XLA Modules:
  0.0 1679.9 jit_solution(2186722558144076932)
XLA Ops:
  6.5 1.1 convert_element_type.42
  7.6 1.7 convolution_bitcast_fusion.13
  9.4 16.2 all_gather.52
  27.1 13.1 all_gather.54
  40.7 34.6 %all-reduce.11.cloned.1.call-done = f32[1,128,128]{1,2,0:T(8,128)} async-done(((f32[1,128,128]{1,2,0:T(8,128)}), f32[1,128,128]{1,2,0:T(8,128)}) %all-reduce.11.cloned.1.call-update) | async-done | bytes 65552 | tf_op jit(solution)/shard_map/psum | solution.py:103
  76.1 3.1 collective-permute-start
  80.2 1.3 collective-permute-start.1
  81.7 4.2 collective-permute-done.1
  86.3 59.3 %psum.134 = f32[128]{0:T(128)S(1)} all-reduce(f32[128]{0:T(128)S(1)} %get-tuple-element.720), channel_id=1, replica_groups=mesh['sec'=32,'blk'=8] {'sec'}, use_global_device_ids=true, to_apply=%region_4.0 | all-reduce | flops 128 | bytes 1024 | tf_op jit(solution)/shard_map/psum | solution.py:122
  145.6 29.8 %psum.135 = f32[128]{0:T(128)S(1)} all-reduce(f32[128]{0:T(128)S(1)} %psum.134), channel_id=1, replica_groups=mesh['sec'=32,'blk'=8] {'blk'}, use_global_device_ids=true, to_apply=%region_5.0 | all-reduce | flops 128 | bytes 1024 | tf_op jit(solution)/shard_map/psum | solution.py:122
  175.6 13.6 all_gather.53
  190.7 62.9 %all-reduce.23.cloned.1.call-done = (f32[128,128]{1,0:T(8,128)}, f32[1,128,128]{2,1,0:T(8,128)}) async-done(((f32[128,128]{1,0:T(8,128)}, f32[1,128,128]{2,1,0:T(8,128)}), (f32[128,128]{1,0:T(8,128)}, f32[1,128,128]{2,1,0:T(8,128)})) %all-reduce.23.cloned.1.call-update) | async-done | bytes 131088 | tf_op jit(solution)/shard_map/psum | solution.py:82
  253.5 1.5 neg.24
  255.7 75.7 %all-gather.12.cloned.1.call-done = f32[4096,128]{1,0:T(8,128)} async-done(((f32[128,128]{1,0:T(8,128)}), f32[4096,128]{1,0:T(8,128)}) %all-gather.12.cloned.1.call-update) | async-done | bytes 2097168 | tf_op jit(solution)/shard_map/all_gather | solution.py:25
  331.4 77.6 %all-gather.6.cloned.1.call-done = f32[32,128,128]{2,1,0:T(8,128)} async-done(((f32[1,128,128]{2,1,0:T(8,128)}), f32[32,128,128]{2,1,0:T(8,128)}) %all-gather.6.cloned.1.call-update) | async-done | bytes 2097168 | tf_op jit(solution)/shard_map/all_gather | solution.py:25
  409.0 63.2 %while.64 = (s32[]{:T(128)}, f32[128,128]{0,1:T(8,128)S(1)}, s32[]{:T(128)}, f32[32,128,128]{2,1,0:T(8,128)}, f32[32,128,128]{2,1,0:T(8,128)}, /*index=5*/s32[]{:T(128)}, s32[]{:T(128)}) while((s32[]{:T(128)}, f32[128,128]{0,1:T(8,128)S(1)}, s32[]{:T(128)}, f32[32,128,128]{2,1,0:T(8,128)}, f32[32,128,128]{2,1,0:T(8,128)}, ...), condition=%wide.region_9.10_spmd.clone, body=%wide.region_8.9_spmd.clone.sunk | while | flops 25231364 | bytes 723043 | solution.py:34
  472.6 17.8 %all_gather.59 = bf16[128,2048]{1,0:T(8,128)(2,1)S(1)} all-gather(bf16[128,256]{1,0:T(8,128)(2,1)S(1)} %get-tuple-element.722), channel_id=1, replica_groups=mesh['sec'=32,'blk'=8] {'blk'}, dimensions={1}, use_global_device_ids=true | all-gather | bytes 589824 | tf_op jit(solution)/shard_map/all_gather | solution.py:101
  491.6 57.6 %all-reduce.13.cloned.1.call-done = f32[1,128,128]{2,1,0:T(8,128)} async-done(((f32[1,128,128]{2,1,0:T(8,128)}), f32[1,128,128]{2,1,0:T(8,128)}) %all-reduce.13.cloned.1.call-update) | async-done | bytes 65552 | tf_op jit(solution)/shard_map/psum | solution.py:103
  550.0 3.1 collective-permute-start.2
  553.6 1.3 collective-permute-start.3
  555.1 4.2 collective-permute-done.3
  559.8 83.2 %psum.139 = f32[1,128]{1,0:T(1,128)S(1)} all-reduce(f32[1,128]{1,0:T(1,128)S(1)} %bitcast.287), channel_id=1, replica_groups=mesh['sec'=32,'blk'=8] {'sec','blk'}, use_global_device_ids=true, to_apply=%region_12.13 | all-reduce | flops 128 | bytes 1024 | tf_op jit(solution)/shard_map/psum | solution.py:151
  643.3 55.8 %psum.140 = f32[128]{0:T(128)S(1)} all-reduce(f32[128]{0:T(128)S(1)} %get-tuple-element.687), channel_id=1, replica_groups=mesh['sec'=32,'blk'=8] {'sec'}, use_global_device_ids=true, to_apply=%region_14.15 | all-reduce | flops 128 | bytes 1024 | tf_op jit(solution)/shard_map/psum | solution.py:122
  699.1 26.6 %psum.141 = f32[128]{0:T(128)S(1)} all-reduce(f32[128]{0:T(128)S(1)} %psum.140), channel_id=1, replica_groups=mesh['sec'=32,'blk'=8] {'blk'}, use_global_device_ids=true, to_apply=%region_15.16 | all-reduce | flops 128 | bytes 1024 | tf_op jit(solution)/shard_map/psum | solution.py:122
  725.8 13.6 all_gather.60
  740.9 57.7 %all-reduce.15.cloned.1.call-done = f32[1,128,128]{2,1,0:T(8,128)} async-done(((f32[1,128,128]{2,1,0:T(8,128)}), f32[1,128,128]{2,1,0:T(8,128)}) %all-reduce.15.cloned.1.call-update) | async-done | bytes 65552 | tf_op jit(solution)/shard_map/psum | solution.py:140
  798.8 77.7 %all-gather.8.cloned.1.call-done = f32[32,128,128]{2,1,0:T(8,128)} async-done(((f32[1,128,128]{2,1,0:T(8,128)}), f32[32,128,128]{2,1,0:T(8,128)}) %all-gather.8.cloned.1.call-update) | async-done | bytes 2097168 | tf_op jit(solution)/shard_map/all_gather | solution.py:25
  876.4 63.2 %while.65 = (s32[]{:T(128)}, f32[128,128]{0,1:T(8,128)S(1)}, s32[]{:T(128)}, f32[32,128,128]{2,1,0:T(8,128)}, f32[32,128,128]{2,1,0:T(8,128)}, /*index=5*/s32[]{:T(128)}, s32[]{:T(128)}) while((s32[]{:T(128)}, f32[128,128]{0,1:T(8,128)S(1)}, s32[]{:T(128)}, f32[32,128,128]{2,1,0:T(8,128)}, f32[32,128,128]{2,1,0:T(8,128)}, ...), condition=%wide.region_18.19_spmd.clone, body=%wide.region_17.18_spmd.clone.sunk | while | flops 25231364 | bytes 723043 | solution.py:34
  879.4 1.1 fusion.164
  881.5 1.1 fusion.164
  887.6 1.1 fusion.164
  895.7 1.1 fusion.164
  903.9 1.1 fusion.164
  912.1 1.1 fusion.164
  920.2 1.1 fusion.164
  928.4 1.1 fusion.164
  936.5 1.1 fusion.164
  940.6 17.8 %all_gather.63 = bf16[128,2048]{1,0:T(8,128)(2,1)S(1)} all-gather(bf16[128,256]{1,0:T(8,128)(2,1)S(1)} %get-tuple-element.724), channel_id=1, replica_groups=mesh['sec'=32,'blk'=8] {'blk'}, dimensions={1}, use_global_device_ids=true | all-gather | bytes 589824 | tf_op jit(solution)/shard_map/all_gather | solution.py:101
  959.6 57.6 %all-reduce.17.cloned.1.call-done = f32[1,128,128]{2,1,0:T(8,128)} async-done(((f32[1,128,128]{2,1,0:T(8,128)}), f32[1,128,128]{2,1,0:T(8,128)}) %all-reduce.17.cloned.1.call-update) | async-done | bytes 65552 | tf_op jit(solution)/shard_map/psum | solution.py:103
  1018.1 3.1 collective-permute-start.4
  1021.7 1.3 collective-permute-start.5
  1023.2 4.2 collective-permute-done.5
  1027.8 83.4 %psum.144 = f32[2,128]{1,0:T(2,128)S(1)} all-reduce(f32[2,128]{1,0:T(2,128)S(1)} %multiply_reduce_fusion.3), channel_id=1, replica_groups=mesh['sec'=32,'blk'=8] {'sec','blk'}, use_global_device_ids=true, to_apply=%region_21.22 | all-reduce | flops 256 | bytes 2048 | tf_op jit(solution)/shard_map/psum | solution.py:151
  1111.5 55.8 %psum.145 = f32[128]{0:T(128)S(1)} all-reduce(f32[128]{0:T(128)S(1)} %get-tuple-element.683), channel_id=1, replica_groups=mesh['sec'=32,'blk'=8] {'sec'}, use_global_device_ids=true, to_apply=%region_24.25 | all-reduce | flops 128 | bytes 1024 | tf_op jit(solution)/shard_map/psum | solution.py:122
  1167.3 26.6 %psum.146 = f32[128]{0:T(128)S(1)} all-reduce(f32[128]{0:T(128)S(1)} %psum.145), channel_id=1, replica_groups=mesh['sec'=32,'blk'=8] {'blk'}, use_global_device_ids=true, to_apply=%region_25.26 | all-reduce | flops 128 | bytes 1024 | tf_op jit(solution)/shard_map/psum | solution.py:122
  1194.1 13.6 all_gather.64
  1209.2 57.8 %all-reduce.19.cloned.1.call-done = f32[1,128,128]{2,1,0:T(8,128)} async-done(((f32[1,128,128]{2,1,0:T(8,128)}), f32[1,128,128]{2,1,0:T(8,128)}) %all-reduce.19.cloned.1.call-update) | async-done | bytes 65552 | tf_op jit(solution)/shard_map/psum | solution.py:140
  1272.3 1.2 scatter.30
  1273.5 71.1 %all-gather.10.cloned.1.call-done = f32[32,128,128]{2,1,0:T(8,128)} async-done(((f32[1,128,128]{2,1,0:T(8,128)}), f32[32,128,128]{2,1,0:T(8,128)}) %all-gather.10.cloned.1.call-update) | async-done | bytes 2097168 | tf_op jit(solution)/shard_map/all_gather | solution.py:25
  1344.6 63.2 %while.66 = (s32[]{:T(128)}, f32[128,128]{0,1:T(8,128)S(1)}, s32[]{:T(128)}, f32[32,128,128]{2,1,0:T(8,128)}, f32[32,128,128]{2,1,0:T(8,128)}, /*index=5*/s32[]{:T(128)}, s32[]{:T(128)}) while((s32[]{:T(128)}, f32[128,128]{0,1:T(8,128)S(1)}, s32[]{:T(128)}, f32[32,128,128]{2,1,0:T(8,128)}, f32[32,128,128]{2,1,0:T(8,128)}, ...), condition=%wide.region_29.30_spmd.clone, body=%wide.region_28.29_spmd.clone.sunk | while | flops 25231364 | bytes 723043 | solution.py:34
  1408.7 17.8 %all_gather.67 = bf16[128,2048]{1,0:T(8,128)(2,1)S(1)} all-gather(bf16[128,256]{1,0:T(8,128)(2,1)S(1)} %get-tuple-element.726), channel_id=1, replica_groups=mesh['sec'=32,'blk'=8] {'blk'}, dimensions={1}, use_global_device_ids=true | all-gather | bytes 589824 | tf_op jit(solution)/shard_map/all_gather | solution.py:101
  1427.7 57.6 %all-reduce.21.cloned.1.call-done = f32[1,128,128]{2,1,0:T(8,128)} async-done(((f32[1,128,128]{2,1,0:T(8,128)}), f32[1,128,128]{2,1,0:T(8,128)}) %all-reduce.21.cloned.1.call-update) | async-done | bytes 65552 | tf_op jit(solution)/shard_map/psum | solution.py:103
  1486.2 3.2 collective-permute-start.6
  1489.9 1.3 collective-permute-start.7
  1491.4 4.2 collective-permute-done.7
  1496.8 83.2 %psum.149 = f32[3,128]{1,0:T(4,128)S(1)} all-reduce(f32[3,128]{1,0:T(4,128)S(1)} %multiply_reduce_fusion.1), channel_id=1, replica_groups=mesh['sec'=32,'blk'=8] {'sec','blk'}, use_global_device_ids=true, to_apply=%region_32.33 | all-reduce | flops 384 | bytes 3072 | tf_op jit(solution)/shard_map/psum | solution.py:151
  1580.2 55.8 %psum.150 = f32[128]{0:T(128)S(1)} all-reduce(f32[128]{0:T(128)S(1)} %multiply_reduce_fusion.4), channel_id=1, replica_groups=mesh['sec'=32,'blk'=8] {'sec'}, use_global_device_ids=true, to_apply=%region_35.36 | all-reduce | flops 128 | bytes 1024 | tf_op jit(solution)/shard_map/psum | solution.py:122
  1636.1 26.6 %psum.151 = f32[128]{0:T(128)S(1)} all-reduce(f32[128]{0:T(128)S(1)} %psum.150), channel_id=1, replica_groups=mesh['sec'=32,'blk'=8] {'blk'}, use_global_device_ids=true, to_apply=%region_36.37 | all-reduce | flops 128 | bytes 1024 | tf_op jit(solution)/shard_map/psum | solution.py:122
  1662.7 1.9 broadcast_select_fusion
  1664.7 1.3 scatter.34
  1666.1 1.8 fusion.80
  1668.0 1.8 broadcast_select_fusion.2
  1669.9 1.8 fusion.76
  1671.7 1.7 add_add_fusion
  (493 shorter events, 204.4 us)
Async XLA Ops:
  6.5 33.7 %copy-start = (bf16[256,2048]{1,0:T(8,128)(2,1)S(1)}, bf16[256,2048]{1,0:T(8,128)(2,1)}, u32[]{:S(2)}) copy-start(bf16[256,2048]{1,0:T(8,128)(2,1)} %param.62) | copy-start | bytes 3145732
  6.5 20.0 %copy-start.1 = (bf16[256,2048]{1,0:T(8,128)(2,1)S(1)}, bf16[256,2048]{1,0:T(8,128)(2,1)}, u32[]{:S(2)}) copy-start(bf16[256,2048]{1,0:T(8,128)(2,1)} %param.61) | copy-start | bytes 3145732
  6.5 20.6 %copy-start.3 = (bf16[256,128]{1,0:T(8,128)(2,1)S(1)}, bf16[256,128]{1,0:T(8,128)(2,1)}, u32[]{:S(2)}) copy-start(bf16[256,128]{1,0:T(8,128)(2,1)} %param.63) | copy-start | bytes 196612
  6.5 68.7 %all-reduce.11.cloned.1.call-start = ((), (), s32[]{:S(2)}) async-start(), calls=%async_computation | async-start | bytes 131072 | tf_op jit(solution)/shard_map/psum | solution.py:103
  9.3 244.2 %all-reduce.23.cloned.1.call-start = ((), (), s32[]{:S(2)}) async-start(), calls=%async_computation.10 | async-start | bytes 262144 | tf_op jit(solution)/shard_map/psum | solution.py:82
  26.6 52.7 %copy-start.9 = (s32[1,128]{1,0:T(1,128)S(1)}, s32[1,128]{1,0:T(1,128)}, u32[]{:S(2)}) copy-start(s32[1,128]{1,0:T(1,128)} %param.65) | copy-start | bytes 1540
  26.6 59.3 %copy-start.2 = (f32[128,256]{1,0:T(8,128)S(1)}, f32[128,256]{1,0:T(8,128)}, u32[]{:S(2)}) copy-start(f32[128,256]{1,0:T(8,128)} %param.58) | copy-start | bytes 393220
  26.6 59.3 %copy-start.8 = (f32[128,256]{1,0:T(8,128)S(1)}, f32[128,256]{1,0:T(8,128)}, u32[]{:S(2)}) copy-start(f32[128,256]{1,0:T(8,128)} %param.59) | copy-start | bytes 393220
  26.6 59.3 %copy-start.10 = (f32[256]{0:T(256)S(1)}, f32[256]{0:T(256)}, u32[]{:S(2)}) copy-start(f32[256]{0:T(256)} %param.60) | copy-start | bytes 3076
  76.1 5.4 collective-permute-start
  80.2 5.7 collective-permute-start.1
  175.5 233.5 %copy-start.11 = (f32[128]{0:T(128)}, f32[128]{0:T(128)S(1)}, u32[]{:S(2)}) copy-start(f32[128]{0:T(128)S(1)} %psum.135) | copy-start | bytes 1540
  190.6 140.8 %all-gather.12.cloned.1.call-start = ((), (), s32[]{:S(2)}) async-start(), calls=%async_computation.9 | async-start | bytes 2162688 | tf_op jit(solution)/shard_map/all_gather | solution.py:25
  255.0 154.0 %all-gather.6.cloned.1.call-start = ((), (), s32[]{:S(2)}) async-start(), calls=%async_computation.1 | async-start | bytes 2162688 | tf_op jit(solution)/shard_map/all_gather | solution.py:25
  255.6 293.6 %all-reduce.13.cloned.1.call-start = ((), (), s32[]{:S(2)}) async-start(), calls=%async_computation.2 | async-start | bytes 131072 | tf_op jit(solution)/shard_map/psum | solution.py:103
  409.0 81.4 %copy-start.7 = (bf16[256,128]{1,0:T(8,128)(2,1)S(1)}, bf16[256,128]{1,0:T(8,128)(2,1)}, u32[]{:S(2)}) copy-start(bf16[256,128]{1,0:T(8,128)(2,1)} %param.64) | copy-start | bytes 196612
  491.2 307.5 %all-reduce.15.cloned.1.call-start = ((), (), s32[]{:S(2)}) async-start(), calls=%async_computation.3 | async-start | bytes 131072 | tf_op jit(solution)/shard_map/psum | solution.py:140
  550.0 4.9 collective-permute-start.2
  553.6 5.7 collective-permute-start.3
  740.9 135.5 %all-gather.8.cloned.1.call-start = ((), (), s32[]{:S(2)}) async-start(), calls=%async_computation.4 | async-start | bytes 2162688 | tf_op jit(solution)/shard_map/all_gather | solution.py:25
  798.7 218.5 %all-reduce.17.cloned.1.call-start = ((), (), s32[]{:S(2)}) async-start(), calls=%async_computation.5 | async-start | bytes 131072 | tf_op jit(solution)/shard_map/psum | solution.py:103
  959.2 307.7 %all-reduce.19.cloned.1.call-start = ((), (), s32[]{:S(2)}) async-start(), calls=%async_computation.6 | async-start | bytes 131072 | tf_op jit(solution)/shard_map/psum | solution.py:140
  1017.2 10.2 copy-start.4
  1018.1 4.9 collective-permute-start.4
  1021.7 5.7 collective-permute-start.5
  1209.1 135.4 %all-gather.10.cloned.1.call-start = ((), (), s32[]{:S(2)}) async-start(), calls=%async_computation.7 | async-start | bytes 2162688 | tf_op jit(solution)/shard_map/all_gather | solution.py:25
  1267.0 218.3 %all-reduce.21.cloned.1.call-start = ((), (), s32[]{:S(2)}) async-start(), calls=%async_computation.8 | async-start | bytes 131072 | tf_op jit(solution)/shard_map/psum | solution.py:103
  1485.3 10.3 copy-start.6
  1486.2 185.5 %copy-start.5 = (f32[128,256]{1,0:T(8,128)S(1)}, f32[128,256]{1,0:T(8,128)}, u32[]{:S(2)}) copy-start(f32[128,256]{1,0:T(8,128)} %get-tuple-element.725) | copy-start | bytes 393220
  1486.2 5.0 collective-permute-start.6
  1489.9 5.7 collective-permute-start.7
Sparse Core Ops, SparseCore 0:
  9.7 65.5 all-reduce.10
  190.7 62.7 all-reduce.22
  256.1 75.2 all-gather.11
  333.8 75.1 all-gather.5
  491.3 57.8 all-reduce.12
  741.0 57.6 all-reduce.14
  801.3 75.1 all-gather.7
  959.3 57.8 all-reduce.16
  1209.2 57.6 all-reduce.18
  1269.4 75.1 all-gather.9
  1427.4 57.8 all-reduce.20
